TPU v7x, 32 devices: a whole 2x2x4 slice. The times are simulated.
32 devices in a mesh: seq: 16 (over z, x, core), head: 2 (over y).
Axes of the slice: x: 2, y: 2, z: 4, core: 2. Of those that a mesh axis runs over, the one named last changes fastest.
Arguments:
- queries: bfloat16 [8192, 8192], P('seq', 'head'), may hold values from -6 to 6
- key_rows: bfloat16 [8192, 8192], P('seq', 'head'), may hold values from -6 to 6
- values: bfloat16 [8192, 8192], P('seq', 'head'), may hold values from -360 to 360
- slopes: float32 [64], P('head'), may hold values from 3.6621094e-05 to 0.06, as said below
- doc_lengths: int32 [8], replicated, may hold values from 1 to 4096, 8192 in all
- norm_gain: float32 [8192], P('head'), may hold values from 0.1 to 1.9
Outputs:
- attended: bfloat16 [8192, 8192], P('seq', 'head')
Inputs may be any that keep to these rules, and one draw needn't show every extreme that they name: `slopes`: each head's rate lies between 0.3 / 8192 and 0.06.
All inputs are finite; a program needn't handle non-finite values.
Results may differ from a plain program's by a relative error of at most 0.0056.
Values may be sent and summed in bfloat16 or wider, within the bound.
A program may use at most 128 MiB of HBM per device.

v0:
```python
import functools

import jax
import jax.numpy as jnp
from jax import lax
from jax.experimental import pallas as pl
from jax.experimental.pallas import tpu as pltpu
from jax.sharding import PartitionSpec as P

BLOCK = 256
FAR = 1e30
LOG2E = 1.4426950408889634
F32 = jnp.float32
BF16 = jnp.bfloat16
MESH = pl.DeviceIdType.MESH


def kernel(
    planes, head_parts, heads, blocks, step, few,
    slopes_ref, docs_ref, q_hbm, k_hbm, v_hbm,
    out_ref, inv_ref,
    q_ref, k_ref, v_ref, mixed_ref, local_ref, own_ref, carry_ref, chip_ref,
    s_send, s_recv, c_send, c_recv, a_send, a_recv, p_send, p_recv, x_send, x_recv,
    lag_ref, same_ref, tail_ref, lead_ref, rem_ref, reach_ref, sq_ref, sq_send, sq_recv,
    q_sem, k_sem, v_sem,
    s_out, s_in, c_out, c_in, a_out, a_in, p_out, p_in, x_out, x_in, sq_out, sq_in,
):
    half = heads // 2
    quarter = half // 2
    parts = half // step
    chunks = 2 * parts
    turns = quarter // few
    rows = blocks * BLOCK
    size = q_ref.shape[1] // heads
    seq = lax.axis_index("seq")
    headpos = lax.axis_index("head")
    core = lax.rem(seq, 2)
    side = lax.rem(lax.div(seq, 2), 2)
    plane = lax.div(seq, 4)
    partner = seq + 1 - 2 * core
    across = seq + 2 - 4 * side
    ahead = jnp.minimum(seq + 4, 4 * planes - 1)
    far = (1 - side) * quarter

    def mine(u):
        return core * half + lax.rem(u + far, half)

    def theirs(u):
        return (1 - core) * half + lax.rem(u + far, half)

    def head_of(o):
        group = jnp.where(o >= half, core, 1 - core)
        return group * half + lax.rem(lax.rem(o, half) + far, half)

    def cols(h):
        return pl.ds(pl.multiple_of(h * size, size), size)

    def wide(oc):
        return pl.ds(pl.multiple_of(head_of(oc * step) * size, step * size), step * size)

    def load(hbm, ref, sem, oc):
        return pltpu.make_async_copy(hbm.at[:, wide(oc)], ref.at[:, wide(oc)], sem.at[oc])

    def remote(src, dst, c, count, out_sem, in_sem, target):
        piece = pl.ds(c * count, count)
        return pltpu.make_async_remote_copy(
            src_ref=src.at[piece], dst_ref=dst.at[piece],
            send_sem=out_sem.at[c], recv_sem=in_sem.at[c],
            device_id={"seq": target}, device_id_type=MESH,
        )

    def s_copy(c):
        return remote(s_send, s_recv, c, step, s_out, s_in, partner)

    def c_copy(c):
        return remote(c_send, c_recv, c, few, c_out, c_in, partner)

    def a_copy(c):
        return remote(a_send, a_recv, c, few, a_out, a_in, across)

    def p_copy(c):
        return remote(p_send, p_recv, c, few, p_out, p_in, ahead)

    def x_copy(c):
        return remote(x_send, x_recv, c, few, x_out, x_in, across)

    def each(count, body, start=0):
        def turn(i, _):
            body(i)
            return 0
        lax.fori_loop(start, count, turn, 0)

    def grouped(c, body, count=step):
        for i in range(count):
            body(c * count + i)

    barrier = pltpu.get_barrier_semaphore()
    pl.semaphore_signal(barrier, inc=1, device_id={"seq": partner}, device_id_type=MESH)
    pl.semaphore_signal(barrier, inc=1, device_id={"seq": across}, device_id_type=MESH)

    @pl.when(plane < planes - 1)
    def _():
        pl.semaphore_signal(barrier, inc=1, device_id={"seq": seq + 4}, device_id_type=MESH)

    @pl.when(plane > 0)
    def _():
        pl.semaphore_signal(barrier, inc=1, device_id={"seq": seq - 4}, device_id_type=MESH)

    for i in range(1, head_parts):
        pl.semaphore_signal(
            barrier, inc=1, device_id={"head": lax.rem(headpos + i, head_parts)}, device_id_type=MESH
        )

    def begin_kv(oc):
        load(k_hbm, k_ref, k_sem, oc).start()
        load(v_hbm, v_ref, v_sem, oc).start()

    each(chunks, begin_kv)
    each(chunks, lambda oc: load(q_hbm, q_ref, q_sem, oc).start())

    starts = []
    total = jnp.int32(0)
    for j in range(docs_ref.shape[0] - 1):
        total = total + docs_ref[j]
        starts.append(total)

    def segment(pos):
        counted = jnp.zeros_like(pos)
        for s in starts:
            counted = counted + jnp.where(pos >= s, 1, 0)
        return jnp.where(pos < 0, -1, counted)

    def joined(a, b):
        return jnp.where(segment(a) == segment(b), F32(1), F32(0))

    base = seq * rows
    chip = base - core * rows
    down = lax.broadcasted_iota(jnp.int32, (BLOCK, BLOCK), 0)
    along = lax.broadcasted_iota(jnp.int32, (BLOCK, BLOCK), 1)
    lag = jnp.where(down >= along, (down - along).astype(F32), F32(FAR))
    lag_ref[...] = lag[BLOCK // 2:]
    offs = lax.broadcasted_iota(jnp.int32, (BLOCK, size), 0)
    rem_ref[...] = (BLOCK - 1 - offs).astype(F32)
    reach_ref[...] = (offs + 1).astype(F32)
    within = []
    for b in range(blocks):
        b0 = base + b * BLOCK
        row_seg = segment(b0 + offs)
        same_ref[b] = jnp.where(segment(b0 + down) == segment(b0 + along), F32(1), F32(0))
        tail_ref[b] = jnp.where(row_seg == segment(b0 + BLOCK - 1), F32(1), F32(0))
        lead_ref[b] = jnp.where(row_seg == segment(b0 - 1), F32(1), F32(0))
        within.append(joined(b0 - 1, b0 + BLOCK - 1))
    board = chip - 2 * side * rows
    j_cores = joined(chip + rows - 1, chip + 2 * rows - 1)
    j_enter = joined(chip - 1, chip + rows - 1)
    j_chips = joined(board + 2 * rows - 1, board + 4 * rows - 1)
    j_board = joined(board - 1, board + 4 * rows - 1)
    j_front = joined(board - 1, board + 2 * rows - 1)

    def rate(h):
        return slopes_ref[h] * F32(-LOG2E)

    def fade(h, distance, keep):
        return jnp.exp2(jnp.full((1, size), rate(h) * distance, F32)) * keep

    sq_ref[...] = jnp.zeros_like(sq_ref)

    @pl.when(plane == 0)
    def _():
        p_recv[...] = jnp.zeros_like(p_recv)

    def end_state(h):
        scale = jnp.exp2(rem_ref[...] * rate(h))
        state = None
        for b in range(blocks):
            here = pl.ds(b * BLOCK, BLOCK)
            weighted = (scale * tail_ref[b] * v_ref[here, cols(h)].astype(F32)).astype(BF16)
            one = lax.dot_general(
                k_ref[here, cols(h)], weighted, (((0,), (0,)), ((), ())), preferred_element_type=F32
            )
            if b < blocks - 1:
                local_ref[b, h] = one
            state = one if state is None else fade(h, F32(BLOCK), within[b]) * state + one
        return state

    def wait_kv(oc):
        load(k_hbm, k_ref, k_sem, oc).wait()
        load(v_hbm, v_ref, v_sem, oc).wait()

    def give(i):
        s_send[i] = end_state(theirs(i)).astype(BF16)

    def keep(i):
        own_ref[i] = end_state(mine(i))

    def first_chunk(c):
        wait_kv(c)
        grouped(c, give)

    first_chunk(jnp.int32(0))
    beside = jnp.where(plane > 0, 1, 0) + jnp.where(plane < planes - 1, 1, 0)
    pl.semaphore_wait(barrier, 1 + head_parts + beside)
    s_copy(0).start()

    def next_chunk(c):
        first_chunk(c)
        s_copy(c).start()

    each(parts, next_chunk, 1)

    def own_chunk(c):
        wait_kv(parts + c)
        grouped(c, keep)

    each(parts, own_chunk)

    mid = BLOCK // 2

    def intra(h):
        decay = jnp.exp2(lag_ref[...] * rate(h))
        for b in range(blocks):
            here = pl.ds(b * BLOCK, BLOCK)
            scores = lax.dot_general(
                q_ref[here, cols(h)], k_ref[here, cols(h)], (((1,), (1,)), ((), ())),
                preferred_element_type=F32,
            )
            upper = (scores[:mid, :mid] * decay[:, mid:] * same_ref[b, :mid, :mid]).astype(BF16)
            lower = (scores[mid:] * decay * same_ref[b, mid:, :]).astype(BF16)
            weights = jnp.concatenate(
                [jnp.concatenate([upper, jnp.zeros((mid, mid), BF16)], axis=1), lower], axis=0
            )
            mixed_ref[here, cols(h)] = jnp.dot(
                weights, v_ref[here, cols(h)], preferred_element_type=F32
            )

    def intra_chunk(oc):
        load(q_hbm, q_ref, q_sem, oc).wait()
        grouped(oc, lambda o: intra(head_of(o)))

    is_second = core == 1
    is_after = side == 1

    def core_states(u):
        here, there = own_ref[u], s_recv[u].astype(F32)
        return jnp.where(is_second, there, here), jnp.where(is_second, here, there)

    def chip_state(u):
        early, late = core_states(u)
        return fade(mine(u), F32(rows), j_cores) * early + late

    def give_chip(w):
        a_send[w] = chip_state(w).astype(BF16)

    def keep_chip(w):
        chip_ref[w] = chip_state(quarter + w)

    def give_chunk(c):
        s_copy(c).wait_recv()
        grouped(c, give_chip)
        for i in range(step // few):
            a_copy(c * (step // few) + i).start()

    each(parts // 2, give_chunk)

    def keep_chunk(c):
        s_copy(parts // 2 + c).wait_recv()
        grouped(c, keep_chip)

    each(parts // 2, keep_chunk)

    def settle(u, enters):
        early, _ = core_states(u)
        second = fade(mine(u), F32(rows), j_enter) * enters + early
        carry_ref[u] = jnp.where(is_second, second, enters)
        c_send[u] = jnp.where(is_second, enters, second).astype(BF16)

    def chain(w):
        h = mine(quarter + w)
        here, there = chip_ref[w], a_recv[w].astype(F32)
        early, late = jnp.where(is_after, there, here), jnp.where(is_after, here, there)
        before = p_recv[w].astype(F32)
        total = fade(h, F32(2 * rows), j_chips) * early + late
        p_send[w] = (fade(h, F32(4 * rows), j_board) * before + total).astype(BF16)
        second = fade(h, F32(2 * rows), j_front) * before + early
        x_send[w] = jnp.where(is_after, before, second).astype(BF16)
        settle(quarter + w, jnp.where(is_after, second, before))

    def chain_chunk(c):
        a_copy(c).wait_recv()

        @pl.when(plane > 0)
        def _():
            p_copy(c).wait_recv()

        grouped(c, chain, few)

        @pl.when(plane < planes - 1)
        def _():
            p_copy(c).start()

        x_copy(c).start()
        c_copy(turns + c).start()

    def across_chunk(c):
        x_copy(c).wait_recv()
        grouped(c, lambda w: settle(w, x_recv[w].astype(F32)), few)
        c_copy(c).start()

    ready = jnp.minimum(2 + 2 * plane, chunks)
    each(ready, intra_chunk)
    each(turns, chain_chunk)
    each(chunks, intra_chunk, ready)
    each(turns, across_chunk)

    def finish_all(work):
        fades = [jnp.exp2(reach_ref[...] * rate(h)) for h, _ in work]
        states = [enters for _, enters in work]
        for b in range(blocks):
            here = pl.ds(b * BLOCK, BLOCK)
            squares = sq_ref[here, :]
            for i, (h, _) in enumerate(work):
                inter = jnp.dot(
                    q_ref[here, cols(h)], states[i].astype(BF16), preferred_element_type=F32
                )
                mixed = mixed_ref[here, cols(h)] + inter * (fades[i] * lead_ref[b])
                squares = squares + mixed * mixed
                out_ref[here, cols(h)] = mixed.astype(BF16)
                if b < blocks - 1:
                    states[i] = fade(h, F32(BLOCK), within[b]) * states[i] + local_ref[b, h]
            sq_ref[here, :] = squares

    def own_part(c):
        finish_all([(mine(c * step + i), carry_ref[c * step + i]) for i in range(step)])

    each(parts, own_part)

    def other_part(c):
        for i in range(step // few):
            c_copy(c * (step // few) + i).wait_recv()
        finish_all(
            [(theirs(c * step + i), c_recv[c * step + i].astype(F32)) for i in range(step)]
        )

    each(parts, other_part)

    ones = jnp.ones((8, size), F32)
    summed = lax.dot_general(
        ones, sq_ref[...], (((1,), (1,)), ((), ())),
        precision=lax.Precision.HIGHEST, preferred_element_type=F32,
    )
    sq_send[...] = summed

    def sq_copy(i):
        return pltpu.make_async_remote_copy(
            src_ref=sq_send, dst_ref=sq_recv.at[i], send_sem=sq_out.at[i], recv_sem=sq_in.at[i],
            device_id={"head": lax.rem(headpos + i, head_parts)}, device_id_type=MESH,
        )

    for i in range(1, head_parts):
        sq_copy(i).start()

    each(parts, lambda c: s_copy(c).wait_send())
    each(2 * turns, lambda c: c_copy(c).wait_send())

    def drain(c):
        a_copy(c).wait_send()
        x_copy(c).wait_send()

        @pl.when(plane < planes - 1)
        def _():
            p_copy(c).wait_send()

    each(turns, drain)
    for i in range(1, head_parts):
        sq_copy(i).wait_recv()
        summed = summed + sq_recv[i]
    inverse = lax.rsqrt(summed / F32(heads * size * head_parts) + F32(1e-05))
    inv_ref[...] = jnp.broadcast_to(jnp.transpose(inverse)[:, 0:1], inv_ref.shape)
    for i in range(1, head_parts):
        sq_copy(i).wait_send()


def scale_kernel(mixed_ref, inv_ref, gain_ref, final_hbm, final_ref, sem):
    rows, size = inv_ref.shape
    strip = rows // sem.shape[0]

    def move(i):
        here = pl.ds(i * strip, strip)
        return pltpu.make_async_copy(final_ref.at[here], final_hbm.at[here], sem.at[i])

    for i in range(sem.shape[0]):
        here = pl.ds(i * strip, strip)
        inverse = inv_ref[here, :]
        for c in range(0, final_ref.shape[1], size):
            piece = mixed_ref[here, c:c + size].astype(F32)
            final_ref[here, c:c + size] = (piece * inverse * gain_ref[:, c:c + size]).astype(BF16)
        move(i).start()
    for i in range(sem.shape[0]):
        move(i).wait()


def shards(planes, head_parts, queries, key_rows, values, slopes, doc_lengths, norm_gain):
    rows, feat = queries.shape
    heads = slopes.shape[0]
    size = feat // heads
    blocks = rows // BLOCK
    half = heads // 2
    quarter = half // 2
    step = min(4, quarter)
    few = max(1, quarter // 8)
    parts = half // step
    turns = quarter // few
    hbm = pl.BlockSpec(memory_space=pltpu.HBM)
    smem = pl.BlockSpec(memory_space=pltpu.SMEM)
    states = lambda count, dtype: pltpu.VMEM((count, size, size), dtype)
    dma = lambda n: pltpu.SemaphoreType.DMA((n,))
    mixed, inverse = pl.pallas_call(
        functools.partial(kernel, planes, head_parts, heads, blocks, step, few),
        out_shape=(
            jax.ShapeDtypeStruct((rows, feat), BF16),
            jax.ShapeDtypeStruct((rows, size), F32),
        ),
        in_specs=[smem, smem, hbm, hbm, hbm],
        out_specs=(pl.BlockSpec(memory_space=pltpu.VMEM), pl.BlockSpec(memory_space=pltpu.VMEM)),
        scratch_shapes=[
            pltpu.VMEM((rows, feat), BF16),
            pltpu.VMEM((rows, feat), BF16),
            pltpu.VMEM((rows, feat), BF16),
            pltpu.VMEM((rows, feat), F32),
            pltpu.VMEM((max(blocks - 1, 1), heads, size, size), F32),
            states(half, F32),
            states(half, F32),
            states(quarter, F32),
            *[states(half, BF16)] * 4,
            *[states(quarter, BF16)] * 6,
            pltpu.VMEM((BLOCK // 2, BLOCK), F32),
            pltpu.VMEM((blocks, BLOCK, BLOCK), F32),
            pltpu.VMEM((blocks, BLOCK, size), F32),
            pltpu.VMEM((blocks, BLOCK, size), F32),
            pltpu.VMEM((BLOCK, size), F32),
            pltpu.VMEM((BLOCK, size), F32),
            pltpu.VMEM((rows, size), F32),
            pltpu.VMEM((8, rows), F32),
            pltpu.VMEM((head_parts, 8, rows), F32),
            *[dma(2 * parts)] * 3,
            *[dma(parts)] * 2,
            *[dma(2 * turns)] * 2,
            *[dma(turns)] * 6,
            dma(head_parts),
            dma(head_parts),
        ],
        compiler_params=pltpu.CompilerParams(
            collective_id=0, has_side_effects=True, vmem_limit_bytes=47 * 1024 * 1024
        ),
    )(slopes, doc_lengths, queries, key_rows, values)
    vmem = pl.BlockSpec(memory_space=pltpu.VMEM)
    return pl.pallas_call(
        scale_kernel,
        out_shape=jax.ShapeDtypeStruct((rows, feat), BF16),
        in_specs=[vmem, vmem, vmem],
        out_specs=pl.BlockSpec(memory_space=pltpu.HBM),
        scratch_shapes=[pltpu.VMEM((rows, feat), BF16), pltpu.SemaphoreType.DMA((8,))],
        compiler_params=pltpu.CompilerParams(vmem_limit_bytes=9 * 1024 * 1024),
    )(mixed, inverse, norm_gain.reshape(1, feat))


def solution(mesh):
    placed = (P("seq", "head"), P("seq", "head"), P("seq", "head"), P("head"), P(), P("head"))
    return jax.shard_map(
        functools.partial(shards, mesh.shape["seq"] // 4, mesh.shape["head"]),
        mesh=mesh, in_specs=placed, out_specs=P("seq", "head"), check_vma=False,
    )
```

profile of v0, /device:TPU:26, one launch (start us, length us, event | category | flops | bytes accessed | tf_op | source)
XLA Modules:
  0.0 37.1 jit_solution(5991985410231173743)
XLA Ops:
  0.0 0.0 copy-start.1
  0.0 0.7 %copy-done.1 = f32[32]{0:T(128)S(1)} copy-done((f32[32]{0:T(128)S(1)}, f32[32]{0:T(128)}, u32[]{:S(2)}) %copy-start.1) | copy-done | bytes 152
  0.7 0.0 copy-start.2
  0.7 0.7 %copy-done.2 = s32[8]{0:T(128)S(1)} copy-done((s32[8]{0:T(128)S(1)}, s32[8]{0:T(128)}, u32[]{:S(2)}) %copy-start.2) | copy-done | bytes 56
  1.3 0.0 copy-start
  1.3 33.5 %shard_map.64 = (bf16[512,4096]{1,0:T(8,128)(2,1)S(1)}, f32[512,128]{1,0:T(8,128)S(1)}) custom-call(f32[32]{0:T(128)S(1)} %copy-done.1, s32[8]{0:T(128)S(1)} %copy-done.2, bf16[512,4096]{1,0:T(8,128)(2,1)} %q_hbm.1, bf16[512,4096]{1,0:T(8,128)(2,1)} %k_hbm.1, bf16[512,4096]{1,0:T(8,128)(2,1)} %v_hbm.1), custom_call_target="tpu_custom_call" | custom-call | tf_op jit(solution)/shard_map/pallas_call | solution.py:417
  34.9 0.0 copy-done
  34.9 2.2 %shard_map.65 = bf16[512,4096]{1,0:T(8,128)(2,1)} custom-call(bf16[512,4096]{1,0:T(8,128)(2,1)S(1)} %get-tuple-element.7.mixed_ref, f32[512,128]{1,0:T(8,128)S(1)} %get-tuple-element.8.inv_ref, f32[1,4096]{1,0:T(1,128)S(1)} %bitcast.1), custom_call_target="tpu_custom_call" | custom-call | tf_op jit(solution)/shard_map/pallas_call | solution.py:457
Async XLA Ops:
  0.0 0.7 %copy-start.1 = (f32[32]{0:T(128)S(1)}, f32[32]{0:T(128)}, u32[]{:S(2)}) copy-start(f32[32]{0:T(128)} %slopes_ref.1) | copy-start | bytes 388
  0.7 0.7 %copy-start.2 = (s32[8]{0:T(128)S(1)}, s32[8]{0:T(128)}, u32[]{:S(2)}) copy-start(s32[8]{0:T(128)} %docs_ref.1) | copy-start | bytes 100
  1.3 33.6 %copy-start = (f32[4096]{0:T(1024)S(1)}, f32[4096]{0:T(1024)}, u32[]{:S(2)}) copy-start(f32[4096]{0:T(1024)} %param.11) | copy-start | bytes 49156
where the time goes:
time: 37.3 us; the launch traced here: 37.1 us
  Pallas kernels  35.8 us (96%)
  local copies, waits for them, and re-layouts  1.31 us (4%)
    pallas_call x1, Pallas kernels, shards(): pl.pallas_call(functools.partial(kernel, planes, head_parts, heads, block...  33.5 us
    pallas_call x1, Pallas kernels, shards(): pl.pallas_call(scale_kernel, out_shape=jax.ShapeDtypeStruct((rows, feat),...  2.21 us
    unnamed x6, local copies, waits for them, and re-layouts  1.31 us

commit v1 on v0

v1 whole, which is shorter than its diff:
```python
import functools

import jax
import jax.numpy as jnp
from jax import lax
from jax.experimental import pallas as pl
from jax.experimental.pallas import tpu as pltpu
from jax.sharding import PartitionSpec as P

BLOCK = 256
FAR = 1e30
LOG2E = 1.4426950408889634
F32 = jnp.float32
BF16 = jnp.bfloat16
MESH = pl.DeviceIdType.MESH
CUT = 1
HOP = 4
XLAG = 4
XTRIP = 4
CTRIP = 2
LATE = 2


def kernel(
    planes, head_parts, heads, blocks,
    slopes_hbm, docs_hbm, q_hbm, k_hbm, v_hbm,
    out_ref, inv_ref,
    q_ref, k_ref, v_ref, mixed_ref, local_ref, even_ref, odd_ref, own_ref, carry_ref, chip_ref,
    s_send, s_recv, c_send, c_recv, a_send, a_recv, p_send, p_recv, x_send, x_recv,
    lag_ref, same_ref, tail_ref, lead_ref, rem_ref, reach_ref, sq_ref, sq_send, sq_recv,
    slopes_ref, docs_ref, small_sem, k_sem, v_sem, q_sem,
    s_out, s_in, c_out, c_in, a_out, a_in, p_out, p_in, x_out, x_in, sq_out, sq_in,
):
    groups = heads // 4
    rows = blocks * BLOCK
    size = q_ref.shape[1] // heads
    piece = size // CUT
    late = min(LATE, groups)

    def load(hbm, ref, sem, w):
        wide = pl.ds(pl.multiple_of(w * 4 * size, 4 * size), 4 * size)
        return pltpu.make_async_copy(hbm.at[:, wide], ref.at[:, wide], sem.at[w])

    def each(count, body, start=0):
        def turn(i, _):
            body(i)
            return 0
        lax.fori_loop(start, count, turn, 0)

    def begin_kv(w):
        load(k_hbm, k_ref, k_sem, w).start()
        load(v_hbm, v_ref, v_sem, w).start()

    slopes_copy = pltpu.make_async_copy(slopes_hbm, slopes_ref, small_sem.at[0])
    docs_copy = pltpu.make_async_copy(docs_hbm, docs_ref, small_sem.at[1])
    begin_kv(0)
    docs_copy.start()
    slopes_copy.start()
    each(groups, begin_kv, 1)
    each(groups, lambda w: load(q_hbm, q_ref, q_sem, w).start())

    seq = lax.axis_index("seq")
    headpos = lax.axis_index("head")
    core = lax.rem(seq, 2)
    side = lax.rem(lax.div(seq, 2), 2)
    plane = lax.div(seq, 4)
    partner = seq + 1 - 2 * core
    across = seq + 2 - 4 * side
    ahead = jnp.minimum(seq + 4, 4 * planes - 1)

    barrier = pltpu.get_barrier_semaphore()
    pl.semaphore_signal(barrier, inc=1, device_id={"seq": partner}, device_id_type=MESH)
    pl.semaphore_signal(barrier, inc=1, device_id={"seq": across}, device_id_type=MESH)

    @pl.when(plane < planes - 1)
    def _():
        pl.semaphore_signal(barrier, inc=1, device_id={"seq": seq + 4}, device_id_type=MESH)

    @pl.when(plane > 0)
    def _():
        pl.semaphore_signal(barrier, inc=1, device_id={"seq": seq - 4}, device_id_type=MESH)

    for i in range(1, head_parts):
        pl.semaphore_signal(
            barrier, inc=1, device_id={"head": lax.rem(headpos + i, head_parts)}, device_id_type=MESH
        )

    def cols(h, wide=1):
        return pl.ds(pl.multiple_of(h * size, wide * size), wide * size)

    def remote(src, dst, first, count, sem_at, out_sem, in_sem, target):
        part = pl.ds(first, count)
        return pltpu.make_async_remote_copy(
            src_ref=src.at[part], dst_ref=dst.at[part],
            send_sem=out_sem.at[sem_at], recv_sem=in_sem.at[sem_at],
            device_id={"seq": target}, device_id_type=MESH,
        )

    def s_copy(w):
        return remote(s_send, s_recv, 2 * w * CUT, 2 * CUT, w, s_out, s_in, partner)

    def c_copy(n):
        return remote(c_send, c_recv, n, 1, n, c_out, c_in, partner)

    def a_copy(j):
        return remote(a_send, a_recv, j, 1, j, a_out, a_in, across)

    def p_copy(j):
        return remote(p_send, p_recv, j, 1, j, p_out, p_in, ahead)

    def x_copy(j):
        return remote(x_send, x_recv, j, 1, j, x_out, x_in, across)

    down = lax.broadcasted_iota(jnp.int32, (BLOCK, BLOCK), 0)
    along = lax.broadcasted_iota(jnp.int32, (BLOCK, BLOCK), 1)
    lag = jnp.where(down >= along, (down - along).astype(F32), F32(FAR))
    lag_ref[...] = lag[BLOCK // 2:]
    offs = lax.broadcasted_iota(jnp.int32, (BLOCK, size), 0)
    rem_ref[...] = (BLOCK - 1 - offs).astype(F32)
    reach_ref[...] = (offs + 1).astype(F32)
    sq_ref[...] = jnp.zeros_like(sq_ref)

    docs_copy.wait()
    slopes_copy.wait()
    starts = []
    total = jnp.int32(0)
    for j in range(docs_ref.shape[0] - 1):
        total = total + docs_ref[j]
        starts.append(total)

    def segment(pos):
        counted = jnp.zeros_like(pos)
        for s in starts:
            counted = counted + jnp.where(pos >= s, 1, 0)
        return jnp.where(pos < 0, -1, counted)

    def joined(a, b):
        return jnp.where(segment(a) == segment(b), F32(1), F32(0))

    base = seq * rows
    chip = base - core * rows
    within = []
    for b in range(blocks):
        b0 = base + b * BLOCK
        row_seg = segment(b0 + offs)
        tail_ref[b] = jnp.where(row_seg == segment(b0 + BLOCK - 1), F32(1), F32(0))
        lead_ref[b] = jnp.where(row_seg == segment(b0 - 1), F32(1), F32(0))
        within.append(joined(b0 - 1, b0 + BLOCK - 1))
    board = chip - 2 * side * rows
    j_cores = joined(chip + rows - 1, chip + 2 * rows - 1)
    j_enter = joined(chip - 1, chip + rows - 1)
    j_chips = joined(board + 2 * rows - 1, board + 4 * rows - 1)
    j_board = joined(board - 1, board + 4 * rows - 1)
    j_front = joined(board - 1, board + 2 * rows - 1)

    def rate(h):
        return slopes_ref[h] * F32(-LOG2E)

    def fade(h, distance, keep):
        return jnp.exp2(jnp.full((1, size), rate(h) * distance, F32)) * keep

    @pl.when(plane == 0)
    def _():
        p_recv[...] = jnp.zeros_like(p_recv)

    def end_state(h):
        scale = jnp.exp2(rem_ref[...] * rate(h))
        state = None
        for b in range(blocks):
            here = pl.ds(b * BLOCK, BLOCK)
            weighted = (scale * tail_ref[b] * v_ref[here, cols(h)].astype(F32)).astype(BF16)
            one = lax.dot_general(
                k_ref[here, cols(h)], weighted, (((0,), (0,)), ((), ())), preferred_element_type=F32
            )
            if b < blocks - 1:
                local_ref[b, h] = one
            state = one if state is None else fade(h, F32(BLOCK), within[b]) * state + one
        return state

    def cut(i):
        return slice(i * piece, (i + 1) * piece)

    def ends(w):
        load(k_hbm, k_ref, k_sem, w).wait()
        load(v_hbm, v_ref, v_sem, w).wait()
        for b0 in range(2):
            state = end_state(4 * w + 2 * (1 - core) + b0).astype(BF16)
            for i in range(CUT):
                s_send[(2 * w + b0) * CUT + i] = state[cut(i)]
        for b0 in range(2):
            state = end_state(4 * w + 2 * core + b0)
            for i in range(CUT):
                own_ref[(2 * w + b0) * CUT + i] = state[cut(i)]

    is_second = core == 1
    is_after = side == 1

    def core_states(n):
        here, there = own_ref[n], s_recv[n].astype(F32)
        return jnp.where(is_second, there, here), jnp.where(is_second, here, there)

    def chip_state(h, n):
        early, late_one = core_states(n)
        return fade(h, F32(rows), j_cores) * early + late_one

    def give_head(w):
        return 4 * w + 2 * core + (1 - side)

    def keep_head(w):
        return 4 * w + 2 * core + side

    def give(w):
        s_copy(w).wait_recv()
        for i in range(CUT):
            n = (2 * w + (1 - side)) * CUT + i
            a_send[w * CUT + i] = chip_state(give_head(w), n).astype(BF16)
        for i in range(CUT):
            a_copy(w * CUT + i).start()
        for i in range(CUT):
            n = (2 * w + side) * CUT + i
            chip_ref[w * CUT + i] = chip_state(keep_head(w), n)

    def settle(h, n, enters):
        early, _ = core_states(n)
        second = fade(h, F32(rows), j_enter) * enters + early
        carry_ref[n] = jnp.where(is_second, second, enters)
        c_send[n] = jnp.where(is_second, enters, second).astype(BF16)
        c_copy(n).start()

    def chain(w):
        h = keep_head(w)
        for i in range(CUT):
            j = w * CUT + i
            a_copy(j).wait_recv()

            @pl.when(plane > 0)
            def _():
                p_copy(j).wait_recv()

            here, there = chip_ref[j], a_recv[j].astype(F32)
            early, late_one = jnp.where(is_after, there, here), jnp.where(is_after, here, there)
            before = p_recv[j].astype(F32)
            total = fade(h, F32(2 * rows), j_chips) * early + late_one
            p_send[j] = (fade(h, F32(4 * rows), j_board) * before + total).astype(BF16)

            @pl.when(plane < planes - 1)
            def _():
                p_copy(j).start()

            second = fade(h, F32(2 * rows), j_front) * before + early
            x_send[j] = jnp.where(is_after, before, second).astype(BF16)

            @pl.when(plane * HOP >= XLAG)
            def _():
                x_copy(j).start()

            settle(h, (2 * w + side) * CUT + i, jnp.where(is_after, second, before))

    def x_start(w):
        for i in range(CUT):
            x_copy(w * CUT + i).start()

    def over(w):
        for i in range(CUT):
            j = w * CUT + i
            x_copy(j).wait_recv()
            settle(give_head(w), (2 * w + (1 - side)) * CUT + i, x_recv[j].astype(F32))

    mid = BLOCK // 2
    for ref in (even_ref, odd_ref):
        for i in range(2):
            for b in range(blocks):
                ref[i, b, :mid, mid:] = jnp.zeros((mid, BLOCK - mid), BF16)

    for b in range(blocks):
        b0 = base + b * BLOCK
        same_ref[b] = jnp.where(segment(b0 + down) == segment(b0 + along), F32(1), F32(0))

    def weigh(u, ref):
        for i in range(2):
            h = 2 * u + i
            decay = jnp.exp2(lag_ref[...] * rate(h))
            for b in range(blocks):
                here = pl.ds(b * BLOCK, BLOCK)
                scores = lax.dot_general(
                    q_ref[here, cols(h)], k_ref[here, cols(h)], (((1,), (1,)), ((), ())),
                    preferred_element_type=F32,
                )
                ref[i, b, :mid, :mid] = (
                    scores[:mid, :mid] * decay[:, mid:] * same_ref[b, :mid, :mid]
                ).astype(BF16)
                ref[i, b, mid:, :] = (scores[mid:] * decay * same_ref[b, mid:, :]).astype(BF16)

    def apply(u, ref):
        for i in range(2):
            h = 2 * u + i
            for b in range(blocks):
                here = pl.ds(b * BLOCK, BLOCK)
                mixed_ref[here, cols(h)] = jnp.dot(
                    ref[i, b], v_ref[here, cols(h)], preferred_element_type=F32
                )

    units = heads // 2

    def intra(u):
        following = jnp.minimum(u + 1, units - 1)

        @pl.when(lax.rem(u, 2) == 0)
        def _():
            weigh(following, odd_ref)
            apply(u, even_ref)

        @pl.when((lax.rem(u, 2) == 1) & (u < units - 1))
        def _():
            load(q_hbm, q_ref, q_sem, lax.div(following, 2)).wait()

        @pl.when(lax.rem(u, 2) == 1)
        def _():
            weigh(following, even_ref)
            apply(u, odd_ref)

    def finish(h, states):
        blank = jnp.zeros((size, size), BF16)
        for b in range(blocks):
            first, second = states[0].astype(BF16), states[1].astype(BF16)
            joint = jnp.concatenate(
                [jnp.concatenate([first, blank], axis=1), jnp.concatenate([blank, second], axis=1)],
                axis=0,
            )
            for r in range(0, BLOCK, BLOCK // 2):
                here = pl.ds(b * BLOCK + r, BLOCK // 2)
                inter = jnp.dot(q_ref[here, cols(h, 2)], joint, preferred_element_type=F32)
                squares = sq_ref[here, :]
                reach = reach_ref[r:r + BLOCK // 2]
                lead = lead_ref[b, r:r + BLOCK // 2]
                for i in range(2):
                    scale = jnp.exp2(reach * rate(h + i)) * lead
                    mixed = mixed_ref[here, cols(h + i)] + inter[:, i * size:(i + 1) * size] * scale
                    squares = squares + mixed * mixed
                    out_ref[here, cols(h + i)] = mixed.astype(BF16)
                sq_ref[here, :] = squares
            if b < blocks - 1:
                states = [
                    fade(h + i, F32(BLOCK), within[b]) * states[i] + local_ref[b, h + i]
                    for i in range(2)
                ]

    def whole(ref, w, b0):
        parts = [ref[(2 * w + b0) * CUT + i] for i in range(CUT)]
        return parts[0] if CUT == 1 else jnp.concatenate(parts, axis=0)

    def mine(w):
        finish(4 * w + 2 * core, [whole(carry_ref, w, b0) for b0 in range(2)])

    def theirs(w):
        for i in range(2 * CUT):
            c_copy(2 * w * CUT + i).wait_recv()
        finish(4 * w + 2 * (1 - core), [whole(c_recv, w, b0).astype(F32) for b0 in range(2)])

    def ends_step(w):
        ends(w)

        @pl.when(w == 0)
        def _():
            beside = jnp.where(plane > 0, 1, 0) + jnp.where(plane < planes - 1, 1, 0)
            pl.semaphore_wait(barrier, 1 + head_parts + beside)

        s_copy(w).start()

        @pl.when(w >= late)
        def _():
            give(w - late)

    each(groups, ends_step)
    load(q_hbm, q_ref, q_sem, 0).wait()
    weigh(jnp.int32(0), even_ref)

    chain_at = HOP * plane
    x_at = jnp.maximum(chain_at, XLAG)
    over_at = x_at + XTRIP
    mine_at = jnp.maximum(over_at, units)
    last_over = max(HOP * (planes - 1), XLAG) + XTRIP
    slots = max(last_over, units) + groups + CTRIP

    def when_in(t, start, count, body):
        @pl.when((t >= start) & (t < start + count))
        def _():
            body(t - start)

    def slot(t):
        when_in(t, 0, late, lambda n: give(groups - late + n))
        when_in(t, chain_at, groups, chain)

        @pl.when(chain_at < XLAG)
        def _():
            when_in(t, x_at, groups, x_start)

        when_in(t, over_at, groups, over)
        when_in(t, 0, units, intra)
        when_in(t, mine_at, groups, mine)
        when_in(t, mine_at + CTRIP, groups, theirs)

    each(slots, slot)

    ones = jnp.ones((8, size), F32)
    summed = lax.dot_general(
        ones, sq_ref[...], (((1,), (1,)), ((), ())),
        precision=lax.Precision.HIGHEST, preferred_element_type=F32,
    )
    sq_send[...] = summed

    def sq_copy(i):
        return pltpu.make_async_remote_copy(
            src_ref=sq_send, dst_ref=sq_recv.at[i], send_sem=sq_out.at[i], recv_sem=sq_in.at[i],
            device_id={"head": lax.rem(headpos + i, head_parts)}, device_id_type=MESH,
        )

    for i in range(1, head_parts):
        sq_copy(i).start()

    each(groups, lambda w: s_copy(w).wait_send())
    each(2 * groups * CUT, lambda n: c_copy(n).wait_send())

    def drain(j):
        a_copy(j).wait_send()
        x_copy(j).wait_send()

        @pl.when(plane < planes - 1)
        def _():
            p_copy(j).wait_send()

    each(groups * CUT, drain)
    for i in range(1, head_parts):
        sq_copy(i).wait_recv()
        summed = summed + sq_recv[i]
    inverse = lax.rsqrt(summed / F32(heads * size * head_parts) + F32(1e-05))
    inv_ref[...] = jnp.broadcast_to(jnp.transpose(inverse)[:, 0:1], inv_ref.shape)
    for i in range(1, head_parts):
        sq_copy(i).wait_send()


def scale_kernel(mixed_ref, inv_ref, gain_ref, final_hbm, final_ref, sem):
    rows, size = inv_ref.shape
    strip = rows // sem.shape[0]

    def move(i):
        here = pl.ds(i * strip, strip)
        return pltpu.make_async_copy(final_ref.at[here], final_hbm.at[here], sem.at[i])

    for i in range(sem.shape[0]):
        here = pl.ds(i * strip, strip)
        inverse = inv_ref[here, :]
        for c in range(0, final_ref.shape[1], size):
            piece = mixed_ref[here, c:c + size].astype(F32)
            final_ref[here, c:c + size] = (piece * inverse * gain_ref[:, c:c + size]).astype(BF16)
        move(i).start()
    for i in range(sem.shape[0]):
        move(i).wait()


def shards(planes, head_parts, queries, key_rows, values, slopes, doc_lengths, norm_gain):
    rows, feat = queries.shape
    heads = slopes.shape[0]
    size = feat // heads
    blocks = rows // BLOCK
    groups = heads // 4
    hbm = pl.BlockSpec(memory_space=pltpu.HBM)
    piece = size // CUT
    states = lambda count, dtype: pltpu.VMEM((count * CUT, piece, size), dtype)
    dma = lambda n: pltpu.SemaphoreType.DMA((n,))
    mixed, inverse = pl.pallas_call(
        functools.partial(kernel, planes, head_parts, heads, blocks),
        out_shape=(
            jax.ShapeDtypeStruct((rows, feat), BF16),
            jax.ShapeDtypeStruct((rows, size), F32),
        ),
        in_specs=[hbm] * 5,
        out_specs=(pl.BlockSpec(memory_space=pltpu.VMEM), pl.BlockSpec(memory_space=pltpu.VMEM)),
        scratch_shapes=[
            pltpu.VMEM((rows, feat), BF16),
            pltpu.VMEM((rows, feat), BF16),
            pltpu.VMEM((rows, feat), BF16),
            pltpu.VMEM((rows, feat), F32),
            pltpu.VMEM((max(blocks - 1, 1), heads, size, size), F32),
            pltpu.VMEM((2, blocks, BLOCK, BLOCK), BF16),
            pltpu.VMEM((2, blocks, BLOCK, BLOCK), BF16),
            states(2 * groups, F32),
            states(2 * groups, F32),
            states(groups, F32),
            *[states(2 * groups, BF16)] * 4,
            *[states(groups, BF16)] * 6,
            pltpu.VMEM((BLOCK // 2, BLOCK), F32),
            pltpu.VMEM((blocks, BLOCK, BLOCK), F32),
            pltpu.VMEM((blocks, BLOCK, size), F32),
            pltpu.VMEM((blocks, BLOCK, size), F32),
            pltpu.VMEM((BLOCK, size), F32),
            pltpu.VMEM((BLOCK, size), F32),
            pltpu.VMEM((rows, size), F32),
            pltpu.VMEM((8, rows), F32),
            pltpu.VMEM((head_parts, 8, rows), F32),
            pltpu.SMEM(slopes.shape, F32),
            pltpu.SMEM(doc_lengths.shape, jnp.int32),
            dma(2),
            *[dma(groups)] * 3,
            *[dma(groups)] * 2,
            *[dma(2 * groups * CUT)] * 2,
            *[dma(groups * CUT)] * 6,
            dma(head_parts),
            dma(head_parts),
        ],
        compiler_params=pltpu.CompilerParams(
            collective_id=0, has_side_effects=True, vmem_limit_bytes=47 * 1024 * 1024
        ),
    )(slopes, doc_lengths, queries, key_rows, values)
    vmem = pl.BlockSpec(memory_space=pltpu.VMEM)
    return pl.pallas_call(
        scale_kernel,
        out_shape=jax.ShapeDtypeStruct((rows, feat), BF16),
        in_specs=[vmem, vmem, vmem],
        out_specs=pl.BlockSpec(memory_space=pltpu.HBM),
        scratch_shapes=[pltpu.VMEM((rows, feat), BF16), pltpu.SemaphoreType.DMA((8,))],
        compiler_params=pltpu.CompilerParams(vmem_limit_bytes=9 * 1024 * 1024),
    )(mixed, inverse, norm_gain.reshape(1, feat))


def solution(mesh):
    placed = (P("seq", "head"), P("seq", "head"), P("seq", "head"), P("head"), P(), P("head"))
    return jax.shard_map(
        functools.partial(shards, mesh.shape["seq"] // 4, mesh.shape["head"]),
        mesh=mesh, in_specs=placed, out_specs=P("seq", "head"), check_vma=False,
    )
```

time: 37.3 us -> 33.7 us (0.903)
  the two profiles are of different devices: /device:TPU:26 before, /device:TPU:0 now
where the time goes in v1:
time: 33.7 us; the launch traced here: 33.6 us
  Pallas kernels  32.2 us (96%)
  local copies, waits for them, and re-layouts  1.31 us (4%)
    pallas_call x1, Pallas kernels, shards(): pl.pallas_call(functools.partial(kernel, planes, head_parts, heads, block...  30 us
    pallas_call x1, Pallas kernels, shards(): pl.pallas_call(scale_kernel, out_shape=jax.ShapeDtypeStruct((rows, feat),...  2.21 us
    unnamed x6, local copies, waits for them, and re-layouts  1.31 us

profile of v1, /device:TPU:0, one launch (start us, length us, event | category | flops | bytes accessed | tf_op | source)
XLA Modules:
  0.0 33.6 jit_solution(15133046372800270350)
XLA Ops:
  0.0 0.0 copy-start.1
  0.0 0.7 %copy-done.1 = f32[32]{0:T(128)S(1)} copy-done((f32[32]{0:T(128)S(1)}, f32[32]{0:T(128)}, u32[]{:S(2)}) %copy-start.1) | copy-done | bytes 152
  0.7 0.0 copy-start.2
  0.7 0.7 %copy-done.2 = s32[8]{0:T(128)S(1)} copy-done((s32[8]{0:T(128)S(1)}, s32[8]{0:T(128)}, u32[]{:S(2)}) %copy-start.2) | copy-done | bytes 56
  1.3 0.0 copy-start
  1.3 30.0 %shard_map.64 = (bf16[512,4096]{1,0:T(8,128)(2,1)S(1)}, f32[512,128]{1,0:T(8,128)S(1)}) custom-call(f32[32]{0:T(128)S(1)} %copy-done.1, s32[8]{0:T(128)S(1)} %copy-done.2, bf16[512,4096]{1,0:T(8,128)(2,1)} %q_hbm.1, bf16[512,4096]{1,0:T(8,128)(2,1)} %k_hbm.1, bf16[512,4096]{1,0:T(8,128)(2,1)} %v_hbm.1), custom_call_target="tpu_custom_call" | custom-call | tf_op jit(solution)/shard_map/pallas_call | solution.py:471
  31.3 0.0 copy-done
  31.3 2.2 %shard_map.65 = bf16[512,4096]{1,0:T(8,128)(2,1)} custom-call(bf16[512,4096]{1,0:T(8,128)(2,1)S(1)} %get-tuple-element.7.mixed_ref, f32[512,128]{1,0:T(8,128)S(1)} %get-tuple-element.8.inv_ref, f32[1,4096]{1,0:T(1,128)S(1)} %bitcast.1), custom_call_target="tpu_custom_call" | custom-call | tf_op jit(solution)/shard_map/pallas_call | solution.py:516
Async XLA Ops:
  0.0 0.7 %copy-start.1 = (f32[32]{0:T(128)S(1)}, f32[32]{0:T(128)}, u32[]{:S(2)}) copy-start(f32[32]{0:T(128)} %slopes_hbm.1) | copy-start | bytes 388
  0.7 0.7 %copy-start.2 = (s32[8]{0:T(128)S(1)}, s32[8]{0:T(128)}, u32[]{:S(2)}) copy-start(s32[8]{0:T(128)} %docs_hbm.1) | copy-start | bytes 100
  1.3 30.0 %copy-start = (f32[4096]{0:T(1024)S(1)}, f32[4096]{0:T(1024)}, u32[]{:S(2)}) copy-start(f32[4096]{0:T(1024)} %param.11) | copy-start | bytes 49156

commit v2 on v1

--- a/solution.py
+++ b/solution.py
@@ -27,7 +27,7 @@
     out_ref, inv_ref,
     q_ref, k_ref, v_ref, mixed_ref, local_ref, even_ref, odd_ref, own_ref, carry_ref, chip_ref,
     s_send, s_recv, c_send, c_recv, a_send, a_recv, p_send, p_recv, x_send, x_recv,
-    lag_ref, same_ref, tail_ref, lead_ref, rem_ref, reach_ref, sq_ref, sq_send, sq_recv,
+    lag_ref, same_ref, tail_ref, lead_ref, sq_ref, sq_send, sq_recv,
     slopes_ref, docs_ref, small_sem, k_sem, v_sem, q_sem,
     s_out, s_in, c_out, c_in, a_out, a_in, p_out, p_in, x_out, x_in, sq_out, sq_in,
 ):
@@ -116,8 +116,8 @@
     lag = jnp.where(down >= along, (down - along).astype(F32), F32(FAR))
     lag_ref[...] = lag[BLOCK // 2:]
     offs = lax.broadcasted_iota(jnp.int32, (BLOCK, size), 0)
-    rem_ref[...] = (BLOCK - 1 - offs).astype(F32)
-    reach_ref[...] = (offs + 1).astype(F32)
+    rem = (BLOCK - 1 - offs).astype(F32)
+    reach = (offs + 1).astype(F32)
     sq_ref[...] = jnp.zeros_like(sq_ref)
 
     docs_copy.wait()
@@ -143,8 +143,8 @@
     for b in range(blocks):
         b0 = base + b * BLOCK
         row_seg = segment(b0 + offs)
-        tail_ref[b] = jnp.where(row_seg == segment(b0 + BLOCK - 1), F32(1), F32(0))
-        lead_ref[b] = jnp.where(row_seg == segment(b0 - 1), F32(1), F32(0))
+        tail_ref[b] = jnp.where(row_seg == segment(b0 + BLOCK - 1), rem, F32(FAR))
+        lead_ref[b] = jnp.where(row_seg == segment(b0 - 1), reach, F32(FAR))
         within.append(joined(b0 - 1, b0 + BLOCK - 1))
     board = chip - 2 * side * rows
     j_cores = joined(chip + rows - 1, chip + 2 * rows - 1)
@@ -164,11 +164,11 @@
         p_recv[...] = jnp.zeros_like(p_recv)
 
     def end_state(h):
-        scale = jnp.exp2(rem_ref[...] * rate(h))
         state = None
         for b in range(blocks):
             here = pl.ds(b * BLOCK, BLOCK)
-            weighted = (scale * tail_ref[b] * v_ref[here, cols(h)].astype(F32)).astype(BF16)
+            scale = jnp.exp2(tail_ref[b] * rate(h))
+            weighted = (scale * v_ref[here, cols(h)].astype(F32)).astype(BF16)
             one = lax.dot_general(
                 k_ref[here, cols(h)], weighted, (((0,), (0,)), ((), ())), preferred_element_type=F32
             )
@@ -276,39 +276,48 @@
         b0 = base + b * BLOCK
         same_ref[b] = jnp.where(segment(b0 + down) == segment(b0 + along), F32(1), F32(0))
 
+    def weigh_one(u, ref, i, b, decay):
+        h = 2 * u + i
+        here = pl.ds(b * BLOCK, BLOCK)
+        scores = lax.dot_general(
+            q_ref[here, cols(h)], k_ref[here, cols(h)], (((1,), (1,)), ((), ())),
+            preferred_element_type=F32,
+        )
+        ref[i, b, :mid, :mid] = (
+            scores[:mid, :mid] * decay[:, mid:] * same_ref[b, :mid, :mid]
+        ).astype(BF16)
+        ref[i, b, mid:, :] = (scores[mid:] * decay * same_ref[b, mid:, :]).astype(BF16)
+
+    def apply_one(u, ref, i, b):
+        h = 2 * u + i
+        here = pl.ds(b * BLOCK, BLOCK)
+        mixed_ref[here, cols(h)] = jnp.dot(
+            ref[i, b], v_ref[here, cols(h)], preferred_element_type=F32
+        )
+
     def weigh(u, ref):
         for i in range(2):
-            h = 2 * u + i
-            decay = jnp.exp2(lag_ref[...] * rate(h))
+            decay = jnp.exp2(lag_ref[...] * rate(2 * u + i))
             for b in range(blocks):
-                here = pl.ds(b * BLOCK, BLOCK)
-                scores = lax.dot_general(
-                    q_ref[here, cols(h)], k_ref[here, cols(h)], (((1,), (1,)), ((), ())),
-                    preferred_element_type=F32,
-                )
-                ref[i, b, :mid, :mid] = (
-                    scores[:mid, :mid] * decay[:, mid:] * same_ref[b, :mid, :mid]
-                ).astype(BF16)
-                ref[i, b, mid:, :] = (scores[mid:] * decay * same_ref[b, mid:, :]).astype(BF16)
+                weigh_one(u, ref, i, b, decay)
 
     def apply(u, ref):
         for i in range(2):
-            h = 2 * u + i
             for b in range(blocks):
-                here = pl.ds(b * BLOCK, BLOCK)
-                mixed_ref[here, cols(h)] = jnp.dot(
-                    ref[i, b], v_ref[here, cols(h)], preferred_element_type=F32
-                )
+                apply_one(u, ref, i, b)
 
     units = heads // 2
+
+    def both(f, fref, u, uref):
+        apply(u, uref)
+        weigh(f, fref)
 
     def intra(u):
         following = jnp.minimum(u + 1, units - 1)
 
         @pl.when(lax.rem(u, 2) == 0)
         def _():
-            weigh(following, odd_ref)
-            apply(u, even_ref)
+            both(following, odd_ref, u, even_ref)
 
         @pl.when((lax.rem(u, 2) == 1) & (u < units - 1))
         def _():
@@ -316,8 +325,7 @@
 
         @pl.when(lax.rem(u, 2) == 1)
         def _():
-            weigh(following, even_ref)
-            apply(u, odd_ref)
+            both(following, even_ref, u, odd_ref)
 
     def finish(h, states):
         blank = jnp.zeros((size, size), BF16)
@@ -331,10 +339,9 @@
                 here = pl.ds(b * BLOCK + r, BLOCK // 2)
                 inter = jnp.dot(q_ref[here, cols(h, 2)], joint, preferred_element_type=F32)
                 squares = sq_ref[here, :]
-                reach = reach_ref[r:r + BLOCK // 2]
                 lead = lead_ref[b, r:r + BLOCK // 2]
                 for i in range(2):
-                    scale = jnp.exp2(reach * rate(h + i)) * lead
+                    scale = jnp.exp2(lead * rate(h + i))
                     mixed = mixed_ref[here, cols(h + i)] + inter[:, i * size:(i + 1) * size] * scale
                     squares = squares + mixed * mixed
                     out_ref[here, cols(h + i)] = mixed.astype(BF16)
@@ -493,8 +500,6 @@
             pltpu.VMEM((blocks, BLOCK, BLOCK), F32),
             pltpu.VMEM((blocks, BLOCK, size), F32),
             pltpu.VMEM((blocks, BLOCK, size), F32),
-            pltpu.VMEM((BLOCK, size), F32),
-            pltpu.VMEM((BLOCK, size), F32),
             pltpu.VMEM((rows, size), F32),
             pltpu.VMEM((8, rows), F32),
             pltpu.VMEM((head_parts, 8, rows), F32),
@@ -511,7 +516,11 @@
         compiler_params=pltpu.CompilerParams(
             collective_id=0, has_side_effects=True, vmem_limit_bytes=47 * 1024 * 1024
         ),
-    )(slopes, doc_lengths, queries, key_rows, values)
+    )(
+        pltpu.with_memory_space_constraint(slopes, pltpu.HBM),
+        pltpu.with_memory_space_constraint(doc_lengths, pltpu.HBM),
+        queries, key_rows, values,
+    )
     vmem = pl.BlockSpec(memory_space=pltpu.VMEM)
     return pl.pallas_call(
         scale_kernel,

time: 33.7 us -> 32 us (0.950)
  local copies, waits for them, and re-layouts: 1.31 us -> 0.01 us
  Pallas kernels: 32.2 us -> 31.8 us
    unnamed x6 -> x2, local copies, waits for them, and re-layouts: 1.31 us -> 0.01 us
    pallas_call x1, Pallas kernels: 30 us -> 29.6 us  [shards(): pl.pallas_call(functools.partial(kernel, planes, head_parts, heads, block...]
where the time goes in v2:
time: 32 us; the launch traced here: 31.8 us
  Pallas kernels  31.8 us (99%)
    pallas_call x1, Pallas kernels, shards(): pl.pallas_call(functools.partial(kernel, planes, head_parts, heads, block...  29.6 us
    pallas_call x1, Pallas kernels, shards(): pl.pallas_call(scale_kernel, out_shape=jax.ShapeDtypeStruct((rows, feat),...  2.21 us

profile of v2, /device:TPU:0, one launch (start us, length us, event | category | flops | bytes accessed | tf_op | source)
XLA Modules:
  0.0 31.8 jit_solution(2751785728985966040)
XLA Ops:
  0.0 0.0 copy-start
  0.0 29.6 %shard_map.64 = (bf16[512,4096]{1,0:T(8,128)(2,1)S(1)}, f32[512,128]{1,0:T(8,128)S(1)}) custom-call(f32[32]{0:T(128)} %slopes_hbm.1, s32[8]{0:T(128)} %docs_hbm.1, bf16[512,4096]{1,0:T(8,128)(2,1)} %q_hbm.1, bf16[512,4096]{1,0:T(8,128)(2,1)} %k_hbm.1, bf16[512,4096]{1,0:T(8,128)(2,1)} %v_hbm.1), custom_call_target="tpu_custom_call" | custom-call | tf_op jit(solution)/shard_map/pallas_call | solution.py:478
  29.6 0.0 copy-done
  29.6 2.2 %shard_map.65 = bf16[512,4096]{1,0:T(8,128)(2,1)} custom-call(bf16[512,4096]{1,0:T(8,128)(2,1)S(1)} %get-tuple-element.7.mixed_ref, f32[512,128]{1,0:T(8,128)S(1)} %get-tuple-element.8.inv_ref, f32[1,4096]{1,0:T(1,128)S(1)} %bitcast.1), custom_call_target="tpu_custom_call" | custom-call | tf_op jit(solution)/shard_map/pallas_call | solution.py:525
Async XLA Ops:
  0.0 29.6 %copy-start = (f32[4096]{0:T(1024)S(1)}, f32[4096]{0:T(1024)}, u32[]{:S(2)}) copy-start(f32[4096]{0:T(1024)} %param.11) | copy-start | bytes 49156

commit v3 on v2

--- a/solution.py
+++ b/solution.py
@@ -14,7 +14,7 @@
 BF16 = jnp.bfloat16
 MESH = pl.DeviceIdType.MESH
 CUT = 1
-HOP = 4
+HOPS = 14
 XLAG = 4
 XTRIP = 4
 CTRIP = 2
@@ -28,7 +28,7 @@
     q_ref, k_ref, v_ref, mixed_ref, local_ref, even_ref, odd_ref, own_ref, carry_ref, chip_ref,
     s_send, s_recv, c_send, c_recv, a_send, a_recv, p_send, p_recv, x_send, x_recv,
     lag_ref, same_ref, tail_ref, lead_ref, sq_ref, sq_send, sq_recv,
-    slopes_ref, docs_ref, small_sem, k_sem, v_sem, q_sem,
+    slopes_ref, docs_ref, small_sem, kv_sem,
     s_out, s_in, c_out, c_in, a_out, a_in, p_out, p_in, x_out, x_in, sq_out, sq_in,
 ):
     groups = heads // 4
@@ -48,8 +48,8 @@
         lax.fori_loop(start, count, turn, 0)
 
     def begin_kv(w):
-        load(k_hbm, k_ref, k_sem, w).start()
-        load(v_hbm, v_ref, v_sem, w).start()
+        load(k_hbm, k_ref, kv_sem, w).start()
+        load(v_hbm, v_ref, kv_sem, w).start()
 
     slopes_copy = pltpu.make_async_copy(slopes_hbm, slopes_ref, small_sem.at[0])
     docs_copy = pltpu.make_async_copy(docs_hbm, docs_ref, small_sem.at[1])
@@ -57,7 +57,6 @@
     docs_copy.start()
     slopes_copy.start()
     each(groups, begin_kv, 1)
-    each(groups, lambda w: load(q_hbm, q_ref, q_sem, w).start())
 
     seq = lax.axis_index("seq")
     headpos = lax.axis_index("head")
@@ -68,6 +67,8 @@
     across = seq + 2 - 4 * side
     ahead = jnp.minimum(seq + 4, 4 * planes - 1)
 
+    chain_at = lax.div(HOPS * plane, 3)
+
     barrier = pltpu.get_barrier_semaphore()
     pl.semaphore_signal(barrier, inc=1, device_id={"seq": partner}, device_id_type=MESH)
     pl.semaphore_signal(barrier, inc=1, device_id={"seq": across}, device_id_type=MESH)
@@ -92,7 +93,7 @@
         part = pl.ds(first, count)
         return pltpu.make_async_remote_copy(
             src_ref=src.at[part], dst_ref=dst.at[part],
-            send_sem=out_sem.at[sem_at], recv_sem=in_sem.at[sem_at],
+            send_sem=out_sem.at[0], recv_sem=in_sem.at[sem_at],
             device_id={"seq": target}, device_id_type=MESH,
         )
 
@@ -100,7 +101,10 @@
         return remote(s_send, s_recv, 2 * w * CUT, 2 * CUT, w, s_out, s_in, partner)
 
     def c_copy(n):
-        return remote(c_send, c_recv, n, 1, n, c_out, c_in, partner)
+        return remote(c_send, c_recv, n, 1, lax.div(n, CUT), c_out, c_in, partner)
+
+    def c_head(n):
+        return remote(c_send, c_recv, n * CUT, CUT, n, c_out, c_in, partner)
 
     def a_copy(j):
         return remote(a_send, a_recv, j, 1, j, a_out, a_in, across)
@@ -181,8 +185,9 @@
         return slice(i * piece, (i + 1) * piece)
 
     def ends(w):
-        load(k_hbm, k_ref, k_sem, w).wait()
-        load(v_hbm, v_ref, v_sem, w).wait()
+        both_wide = pl.ds(0, 8 * size)
+        pltpu.make_async_copy(k_hbm.at[:, both_wide], k_ref.at[:, both_wide], kv_sem.at[w]).wait()
+        load(q_hbm, q_ref, kv_sem, w).start()
         for b0 in range(2):
             state = end_state(4 * w + 2 * (1 - core) + b0).astype(BF16)
             for i in range(CUT):
@@ -250,7 +255,7 @@
             second = fade(h, F32(2 * rows), j_front) * before + early
             x_send[j] = jnp.where(is_after, before, second).astype(BF16)
 
-            @pl.when(plane * HOP >= XLAG)
+            @pl.when(chain_at >= XLAG)
             def _():
                 x_copy(j).start()
 
@@ -321,13 +326,13 @@
 
         @pl.when((lax.rem(u, 2) == 1) & (u < units - 1))
         def _():
-            load(q_hbm, q_ref, q_sem, lax.div(following, 2)).wait()
+            load(q_hbm, q_ref, kv_sem, lax.div(following, 2)).wait()
 
         @pl.when(lax.rem(u, 2) == 1)
         def _():
             both(following, even_ref, u, odd_ref)
 
-    def finish(h, states):
+    def finish(pair, states):
         blank = jnp.zeros((size, size), BF16)
         for b in range(blocks):
             first, second = states[0].astype(BF16), states[1].astype(BF16)
@@ -337,18 +342,19 @@
             )
             for r in range(0, BLOCK, BLOCK // 2):
                 here = pl.ds(b * BLOCK + r, BLOCK // 2)
-                inter = jnp.dot(q_ref[here, cols(h, 2)], joint, preferred_element_type=F32)
+                both_q = jnp.concatenate([q_ref[here, cols(h)] for h in pair], axis=1)
+                inter = jnp.dot(both_q, joint, preferred_element_type=F32)
                 squares = sq_ref[here, :]
                 lead = lead_ref[b, r:r + BLOCK // 2]
                 for i in range(2):
-                    scale = jnp.exp2(lead * rate(h + i))
-                    mixed = mixed_ref[here, cols(h + i)] + inter[:, i * size:(i + 1) * size] * scale
+                    scale = jnp.exp2(lead * rate(pair[i]))
+                    mixed = mixed_ref[here, cols(pair[i])] + inter[:, i * size:(i + 1) * size] * scale
                     squares = squares + mixed * mixed
-                    out_ref[here, cols(h + i)] = mixed.astype(BF16)
+                    out_ref[here, cols(pair[i])] = mixed.astype(BF16)
                 sq_ref[here, :] = squares
             if b < blocks - 1:
                 states = [
-                    fade(h + i, F32(BLOCK), within[b]) * states[i] + local_ref[b, h + i]
+                    fade(pair[i], F32(BLOCK), within[b]) * states[i] + local_ref[b, pair[i]]
                     for i in range(2)
                 ]
 
@@ -356,13 +362,18 @@
         parts = [ref[(2 * w + b0) * CUT + i] for i in range(CUT)]
         return parts[0] if CUT == 1 else jnp.concatenate(parts, axis=0)
 
-    def mine(w):
-        finish(4 * w + 2 * core, [whole(carry_ref, w, b0) for b0 in range(2)])
-
-    def theirs(w):
-        for i in range(2 * CUT):
-            c_copy(2 * w * CUT + i).wait_recv()
-        finish(4 * w + 2 * (1 - core), [whole(c_recv, w, b0).astype(F32) for b0 in range(2)])
+    def finish_pair(w, b0):
+        c_head(2 * w + b0).wait_recv()
+        finish(
+            (4 * w + 2 * core + b0, 4 * w + 2 * (1 - core) + b0),
+            [whole(carry_ref, w, b0), whole(c_recv, w, b0).astype(F32)],
+        )
+
+    def kept(w):
+        finish_pair(w, side)
+
+    def given(w):
+        finish_pair(w, 1 - side)
 
     def ends_step(w):
         ends(w)
@@ -379,34 +390,38 @@
             give(w - late)
 
     each(groups, ends_step)
-    load(q_hbm, q_ref, q_sem, 0).wait()
-    weigh(jnp.int32(0), even_ref)
-
-    chain_at = HOP * plane
     x_at = jnp.maximum(chain_at, XLAG)
-    over_at = x_at + XTRIP
-    mine_at = jnp.maximum(over_at, units)
-    last_over = max(HOP * (planes - 1), XLAG) + XTRIP
-    slots = max(last_over, units) + groups + CTRIP
+    over_at = jnp.minimum(x_at + XTRIP + 2, jnp.maximum(x_at + XTRIP, units - 2))
+    kept_at = jnp.maximum(chain_at + CTRIP, units)
+    given_at = jnp.maximum(over_at + CTRIP, units + 1)
+    last_x = max(HOPS * (planes - 1) // 3, XLAG)
+    last_over = min(last_x + XTRIP + 2, max(last_x + XTRIP, units - 2))
+    slots = max(last_over + CTRIP, units + 1) + groups
 
     def when_in(t, start, count, body):
         @pl.when((t >= start) & (t < start + count))
         def _():
             body(t - start)
 
-    def slot(t):
+    def hand_on(t):
         when_in(t, 0, late, lambda n: give(groups - late + n))
         when_in(t, chain_at, groups, chain)
 
+    def slot(t):
+        hand_on(t)
+
         @pl.when(chain_at < XLAG)
         def _():
             when_in(t, x_at, groups, x_start)
 
         when_in(t, over_at, groups, over)
         when_in(t, 0, units, intra)
-        when_in(t, mine_at, groups, mine)
-        when_in(t, mine_at + CTRIP, groups, theirs)
-
+
+        when_in(t, kept_at, groups, kept)
+        when_in(t, given_at, groups, given)
+
+    load(q_hbm, q_ref, kv_sem, 0).wait()
+    weigh(jnp.int32(0), even_ref)
     each(slots, slot)
 
     ones = jnp.ones((8, size), F32)
@@ -418,28 +433,27 @@
 
     def sq_copy(i):
         return pltpu.make_async_remote_copy(
-            src_ref=sq_send, dst_ref=sq_recv.at[i], send_sem=sq_out.at[i], recv_sem=sq_in.at[i],
+            src_ref=sq_send, dst_ref=sq_recv.at[i - 1],
+            send_sem=sq_out.at[i - 1], recv_sem=sq_in.at[i - 1],
             device_id={"head": lax.rem(headpos + i, head_parts)}, device_id_type=MESH,
         )
 
     for i in range(1, head_parts):
         sq_copy(i).start()
 
-    each(groups, lambda w: s_copy(w).wait_send())
-    each(2 * groups * CUT, lambda n: c_copy(n).wait_send())
-
-    def drain(j):
-        a_copy(j).wait_send()
-        x_copy(j).wait_send()
-
-        @pl.when(plane < planes - 1)
-        def _():
-            p_copy(j).wait_send()
-
-    each(groups * CUT, drain)
+    count = groups * CUT
+    remote(s_send, s_recv, 0, 2 * count, 0, s_out, s_in, partner).wait_send()
+    remote(c_send, c_recv, 0, 2 * count, 0, c_out, c_in, partner).wait_send()
+    remote(a_send, a_recv, 0, count, 0, a_out, a_in, across).wait_send()
+    remote(x_send, x_recv, 0, count, 0, x_out, x_in, across).wait_send()
+
+    @pl.when(plane < planes - 1)
+    def _():
+        remote(p_send, p_recv, 0, count, 0, p_out, p_in, ahead).wait_send()
+
     for i in range(1, head_parts):
         sq_copy(i).wait_recv()
-        summed = summed + sq_recv[i]
+        summed = summed + sq_recv[i - 1]
     inverse = lax.rsqrt(summed / F32(heads * size * head_parts) + F32(1e-05))
     inv_ref[...] = jnp.broadcast_to(jnp.transpose(inverse)[:, 0:1], inv_ref.shape)
     for i in range(1, head_parts):
@@ -502,16 +516,15 @@
             pltpu.VMEM((blocks, BLOCK, size), F32),
             pltpu.VMEM((rows, size), F32),
             pltpu.VMEM((8, rows), F32),
-            pltpu.VMEM((head_parts, 8, rows), F32),
+            pltpu.VMEM((max(head_parts - 1, 1), 8, rows), F32),
             pltpu.SMEM(slopes.shape, F32),
             pltpu.SMEM(doc_lengths.shape, jnp.int32),
             dma(2),
-            *[dma(groups)] * 3,
-            *[dma(groups)] * 2,
-            *[dma(2 * groups * CUT)] * 2,
-            *[dma(groups * CUT)] * 6,
-            dma(head_parts),
-            dma(head_parts),
+            dma(groups),
+            dma(1), dma(groups),
+            dma(1), dma(2 * groups),
+            *[dma(1), dma(groups * CUT)] * 3,
+            *[dma(max(head_parts - 1, 1))] * 2,
         ],
         compiler_params=pltpu.CompilerParams(
             collective_id=0, has_side_effects=True, vmem_limit_bytes=47 * 1024 * 1024

time: 32 us -> 30.2 us (0.944)
  Pallas kernels: 31.8 us -> 29.9 us
    pallas_call x1, Pallas kernels: 29.6 us -> 27.7 us  [shards(): pl.pallas_call(functools.partial(kernel, planes, head_parts, heads, block...]
where the time goes in v3:
time: 30.2 us; the launch traced here: 30 us
  Pallas kernels  29.9 us (99%)
    pallas_call x1, Pallas kernels, shards(): pl.pallas_call(functools.partial(kernel, planes, head_parts, heads, block...  27.7 us
    pallas_call x1, Pallas kernels, shards(): pl.pallas_call(scale_kernel, out_shape=jax.ShapeDtypeStruct((rows, feat),...  2.21 us

profile of v3, /device:TPU:0, one launch (start us, length us, event | category | flops | bytes accessed | tf_op | source)
XLA Modules:
  0.0 30.0 jit_solution(4892005095047701254)
XLA Ops:
  0.0 0.0 copy-start
  0.0 27.7 %shard_map.64 = (bf16[512,4096]{1,0:T(8,128)(2,1)S(1)}, f32[512,128]{1,0:T(8,128)S(1)}) custom-call(f32[32]{0:T(128)} %slopes_hbm.1, s32[8]{0:T(128)} %docs_hbm.1, bf16[512,4096]{1,0:T(8,128)(2,1)} %q_hbm.1, bf16[512,4096]{1,0:T(8,128)(2,1)} %k_hbm.1, bf16[512,4096]{1,0:T(8,128)(2,1)} %v_hbm.1), custom_call_target="tpu_custom_call" | custom-call | tf_op jit(solution)/shard_map/pallas_call | solution.py:492
  27.7 0.0 copy-done
  27.7 2.2 %shard_map.65 = bf16[512,4096]{1,0:T(8,128)(2,1)} custom-call(bf16[512,4096]{1,0:T(8,128)(2,1)S(1)} %get-tuple-element.7.mixed_ref, f32[512,128]{1,0:T(8,128)S(1)} %get-tuple-element.8.inv_ref, f32[1,4096]{1,0:T(1,128)S(1)} %bitcast.1), custom_call_target="tpu_custom_call" | custom-call | tf_op jit(solution)/shard_map/pallas_call | solution.py:538
Async XLA Ops:
  0.0 27.7 %copy-start = (f32[4096]{0:T(1024)S(1)}, f32[4096]{0:T(1024)}, u32[]{:S(2)}) copy-start(f32[4096]{0:T(1024)} %param.11) | copy-start | bytes 49156
